TPU v7x, 512 devices: a whole 4x8x8 slice. The times are simulated.
512 devices in a mesh: seq: 32 (over z_lo, y), tp: 16 (over x, z_hi, core).
Axes of the slice: x: 4, y: 8, z: 8 (z_hi: 2, z_lo: 4; z = z_hi * 4 + z_lo), core: 2. Of those that a mesh axis runs over, the one named last changes fastest.
Arguments:
- latents: bfloat16 [4096, 3072], P('seq', 'tp'), may hold values from -6 to 6
- lengths: int32 [2], replicated, may hold values from 1 to 3072, 4096 in all
- t_index: int32 [2], replicated, may hold values from 0 to 6
- mod_scale: float32 [3072], replicated, may hold values from -2 to 2
- q_weight: bfloat16 [3072, 2048], P(None, 'tp'), may hold values from -0.109375 to 0.109375
- k_weight: bfloat16 [3072, 2048], P(None, 'tp'), may hold values from -0.109375 to 0.109375
- v_weight: bfloat16 [3072, 2048], P(None, 'tp'), may hold values from -0.109375 to 0.109375
- out_weight: bfloat16 [2048, 3072], P('tp'), may hold values from -0.1875 to 0.1875
- q_gain: float32 [128], replicated, may hold values from 0.6 to 2.4
- k_gain: float32 [128], replicated, may hold values from 0.6 to 2.4
- student_weight: bfloat16 [3072, 3072], P('tp'), may hold values from -0.15625 to 0.15625
Outputs:
- target: bfloat16 [4096, 3072], P('seq', 'tp')
- student_velocity: bfloat16 [4096, 3072], P('seq', 'tp')
- loss: float32 [], replicated
Inputs may be any that keep to these rules, and one draw needn't show every extreme that they name: lengths sum to 4096.
All inputs are finite; a program needn't handle non-finite values.
Results may differ from a plain program's by a relative error of at most 0.024.
Values may be sent and summed in bfloat16 or wider, within the bound.
A program may use at most 64 MiB of HBM per device.

v0:
```python
import functools
import math
import jax
import jax.numpy as jnp
from jax import lax
from jax.sharding import Mesh
from jax.sharding import PartitionSpec as P

TGRID = 8
SEQ = ("seq_0", "seq_1")
TP = ("tp_0", "tp_1", "tp_2")
SEQ_TP = ("seq_0", "seq_1", "tp_0", "tp_1", "tp_2")
epsilon = 1e-06
kinetic_weight = 0.1


def in_one_piece(arrays, axis, dim, along):
    widths = [a.shape[along] for a in arrays]
    both = jnp.concatenate(arrays, axis=along)
    whole = lax.all_gather(both, axis, axis=dim, tiled=True)
    return tuple(jnp.split(whole, [sum(widths[:k]) for k in range(1, len(widths))], axis=along))


def from_everyone(value, axis):
    length = lax.axis_size(axis)
    return lax.all_to_all(
        jnp.broadcast_to(value[None], (length, *value.shape)), axis, 0, 0, tiled=True
    )


def laid_out(pieces, dim):
    pieces = jnp.moveaxis(pieces, 0, dim)
    lengths = pieces.shape
    return pieces.reshape(*lengths[:dim], lengths[dim] * lengths[dim + 1], *lengths[dim + 2 :])


def gathered_copies(value, axis, dim):
    pieces = from_everyone(value, axis)
    return laid_out(pieces, dim)


def over_axes(value, axes):
    return functools.reduce(lax.psum, axes, value)


def image_index(positions, image_ends):
    return jnp.sum((positions[:, None] >= image_ends[None, :]).astype(jnp.int32), axis=1)


def head_norm(projected, gain):
    shaped = projected.reshape(projected.shape[0], -1, gain.shape[0])
    normed = shaped * lax.rsqrt(jnp.mean(shaped * shaped, axis=-1, keepdims=True) + epsilon) * gain
    return normed.astype(jnp.bfloat16)


def grouped_columns(whole_left, right_columns, groups):
    row_count = whole_left.shape[0]
    group_width = whole_left.shape[1] // groups
    left_groups = whole_left.reshape(row_count, groups, group_width)
    right_groups = right_columns.reshape(groups, group_width, right_columns.shape[1])
    terms = jnp.einsum(
        "tng,ngd->tnd", left_groups, right_groups, preferred_element_type=jnp.float32
    ).astype(jnp.bfloat16)
    terms = lax.optimization_barrier(terms)
    return jnp.sum(terms.astype(jnp.float32), axis=1)


def teacher(
    state, times, query_image, image_ends, mod_scale, q_weight, k_weight, v_weight, q_gain, k_gain
):
    row_count = state.shape[0]
    head_dim = q_gain.shape[0]
    state32 = state.astype(jnp.float32)
    normed = state32 * lax.rsqrt(jnp.mean(state32 * state32, axis=1, keepdims=True) + epsilon)
    hidden = (normed * (1.0 + times[:, None] * mod_scale[None, :])).astype(jnp.bfloat16)
    queries = head_norm(jnp.dot(hidden, q_weight, preferred_element_type=jnp.float32), q_gain)
    key_rows = head_norm(jnp.dot(hidden, k_weight, preferred_element_type=jnp.float32), k_gain)
    key_rows = key_rows.reshape(row_count, -1)
    value_rows = jnp.dot(hidden, v_weight, preferred_element_type=jnp.float32).astype(jnp.bfloat16)
    heads_here = queries.shape[1]
    score_scale = 1.0 / math.sqrt(head_dim)
    key_block, value_block = in_one_piece((key_rows, value_rows), SEQ, 0, 1)
    running_max = jnp.full((row_count, heads_here), -1e30, jnp.float32)
    count = key_block.shape[0]
    key_image = image_index(jnp.arange(count, dtype=jnp.int32), image_ends)
    key_heads = key_block.reshape(count, heads_here, head_dim)
    value_heads = value_block.reshape(count, heads_here, head_dim)
    same_image = (query_image[:, None] == key_image[None, :])[:, None, :]
    scores = (
        jnp.einsum("qhd,khd->qhk", queries, key_heads, preferred_element_type=jnp.float32)
        * score_scale
    )
    scores = jnp.where(same_image, scores, -1e30)
    new_max = jnp.maximum(running_max, jnp.max(scores, axis=2))
    weights = jnp.where(same_image, jnp.exp(scores - new_max[:, :, None]), 0.0)
    new_total = jnp.sum(weights, axis=2)
    product = jnp.einsum(
        "qhk,khd->qhd",
        weights.astype(jnp.bfloat16),
        value_heads,
        preferred_element_type=jnp.float32,
    )
    mixed = (product / new_total[:, :, None]).astype(jnp.bfloat16).reshape(row_count, -1)
    return (mixed, hidden)


def on_device(
    latents,
    lengths,
    t_index,
    mod_scale,
    q_weight,
    k_weight,
    v_weight,
    out_weight,
    q_gain,
    k_gain,
    student_weight,
):
    row_count, width_here = latents.shape
    tp_count = lax.axis_size(TP)
    image_ends = jnp.cumsum(lengths)
    row_offset = lax.axis_index(SEQ) * row_count
    query_image = image_index(row_offset + jnp.arange(row_count, dtype=jnp.int32), image_ends)
    one_hot = (
        query_image[:, None] == jnp.arange(lengths.shape[0], dtype=jnp.int32)[None, :]
    ).astype(jnp.float32)
    start_times = jnp.sum(one_hot * (t_index.astype(jnp.float32) / TGRID)[None, :], axis=1)
    step_size = 1.0 / TGRID
    whole_rows = lax.all_gather(latents, TP, axis=1, tiled=True)
    velocities = []
    first_hidden = whole_rows
    out_columns, student_columns = (
        lax.all_to_all(out_weight, TP, split_axis=1, concat_axis=0, tiled=True),
        lax.all_to_all(student_weight, TP, split_axis=1, concat_axis=0, tiled=True),
    )
    state_shard = latents
    for euler_index in range(2):
        if euler_index == 1:
            whole_rows = lax.all_gather(state_shard, TP, axis=1, tiled=True)
        mixed, hidden = teacher(
            whole_rows,
            start_times + euler_index * step_size,
            query_image,
            image_ends,
            mod_scale,
            q_weight,
            k_weight,
            v_weight,
            q_gain,
            k_gain,
        )
        if euler_index == 0:
            first_hidden = hidden
        all_heads = gathered_copies(mixed, TP, 1)
        velocity = grouped_columns(all_heads, out_columns, tp_count).astype(jnp.bfloat16)
        velocities.append(velocity)
        state_shard = (
            latents.astype(jnp.float32) + step_size * velocity.astype(jnp.float32)
        ).astype(jnp.bfloat16)
    student_velocity = grouped_columns(first_hidden, student_columns, tp_count).astype(jnp.bfloat16)
    target = (0.5 * (velocities[0].astype(jnp.float32) + velocities[1].astype(jnp.float32))).astype(
        jnp.bfloat16
    )
    student32 = student_velocity.astype(jnp.float32)
    residual = student32 - target.astype(jnp.float32)
    per_token = jnp.sum(residual * residual, axis=1) + kinetic_weight * jnp.sum(
        student32 * student32, axis=1
    )
    image_part = jnp.sum(one_hot * per_token[:, None], axis=0)
    image_sum = over_axes(image_part, SEQ_TP)
    loss = jnp.mean(image_sum / (lengths.astype(jnp.float32) * mod_scale.shape[0]))
    return (target, student_velocity, loss)


def solution(mesh):
    torus = Mesh(mesh.devices.reshape(4, 8, 4, 2, 2), ("seq_0", "seq_1", "tp_0", "tp_1", "tp_2"))
    in_specs = (
        P(SEQ, TP),
        P(),
        P(),
        P(),
        P(None, TP),
        P(None, TP),
        P(None, TP),
        P(TP, None),
        P(),
        P(),
        P(TP, None),
    )
    out_specs = (P(SEQ, TP), P(SEQ, TP), P())
    return jax.shard_map(
        on_device, mesh=torus, in_specs=in_specs, out_specs=out_specs, check_vma=False
    )
```

profile of v0, /device:TPU:1, one launch (start us, length us, event | category | flops | bytes accessed | tf_op | source)
XLA Modules:
  0.0 472.0 jit_solution(12956411148066289239)
XLA Ops:
  7.2 46.2 %all_gather.12 = bf16[128,3072]{0,1:T(8,128)(2,1)S(1)} all-gather(bf16[128,192]{0,1:T(8,128)(2,1)} %param.11), channel_id=1, replica_groups=mesh['seq_0'=4,'seq_1'=8,'tp_0'=4,'tp_1'=2,'tp_2'=2] {'tp_0','tp_1','tp_2'}, dimensions={1}, use_global_device_ids=true | all-gather | bytes 835584 | tf_op jit(solution)/shard_map/all_gather | solution.py:130
  53.5 0.7 convert_multiply_fusion.6
  54.1 0.4 fusion.8
  54.6 0.8 reduce-window.8
  55.6 1.2 fusion.10
  56.8 0.4 convolution_convert_fusion.3
  57.2 0.4 multiply_reduce_fusion.3
  57.8 0.6 pad_maximum_fusion
  58.4 1.2 copy.19
  59.6 3.6 all-to-all-start.1
  63.2 1.6 multiply_reduce_fusion.2
  64.7 0.1 fusion.57
  64.9 99.5 %all-gather.3.cloned.1.call-done = bf16[4096,256]{0,1:T(8,128)(2,1)} async-done(((bf16[128,256]{0,1:T(8,128)(2,1)}), bf16[4096,256]{0,1:T(8,128)(2,1)}) %all-gather.3.cloned.1.call-update) | async-done | bytes 2097168 | tf_op jit(solution)/shard_map/all_gather | solution.py:20
  164.3 2.3 fusion.72
  166.6 1.9 fusion.4
  168.5 0.9 fusion.29
  169.5 0.9 broadcast_in_dim.20
  170.5 25.1 %all-to-all-start = ((bf16[16,128,128]{2,1,0:T(8,128)(2,1)}), bf16[16,128,128]{2,1,0:T(8,128)(2,1)}, u32[]{:S(2)}, u32[]{:S(2)}) async-start(bf16[16,128,128]{2,1,0:T(8,128)(2,1)} %broadcast_in_dim.20), calls=%async_computation | async-start | bytes 1048576 | tf_op jit(solution)/shard_map/all_to_all | solution.py:26
  195.7 16.0 %all-to-all-done = bf16[16,128,128]{2,1,0:T(8,128)(2,1)} async-done(((bf16[16,128,128]{2,1,0:T(8,128)(2,1)}), bf16[16,128,128]{2,1,0:T(8,128)(2,1)}, u32[]{:S(2)}, u32[]{:S(2)}) %all-to-all-start) | async-done | bytes 524320 | tf_op jit(solution)/shard_map/all_to_all | solution.py:26
  211.7 1.5 fusion.19
  213.2 0.1 reduce_sum.182
  213.3 33.6 %all_gather.14 = bf16[128,3072]{0,1:T(8,128)(2,1)S(1)} all-gather(bf16[128,192]{0,1:T(8,128)(2,1)S(1)} %fusion.51), channel_id=1, replica_groups=mesh['seq_0'=4,'seq_1'=8,'tp_0'=4,'tp_1'=2,'tp_2'=2] {'tp_0','tp_1','tp_2'}, dimensions={1}, use_global_device_ids=true | all-gather | bytes 835584 | tf_op jit(solution)/shard_map/all_gather | solution.py:140
  246.9 0.4 fusion.11
  247.3 2.0 convolution_convert_fusion.2
  249.3 0.9 multiply_reduce_fusion.1
  250.3 0.6 pad_maximum_fusion.1
  250.9 2.5 copy.21
  253.5 9.4 %all-to-all-start.3 = ((bf16[192,16,192]{0,2,1:T(8,128)(2,1)}), bf16[192,16,192]{0,2,1:T(8,128)(2,1)}, u32[]{:S(2)}, u32[]{:S(2)}) async-start(bf16[192,16,192]{0,2,1:T(8,128)(2,1)} %bitcast.82), calls=%async_computation.3 | async-start | bytes 3145728 | tf_op jit(solution)/shard_map/all_to_all | solution.py:135
  262.8 2.0 multiply_reduce_fusion
  264.8 98.7 %all-gather.5.cloned.1.call-done = bf16[4096,256]{0,1:T(8,128)(2,1)} async-done(((bf16[128,256]{0,1:T(8,128)(2,1)}), bf16[4096,256]{0,1:T(8,128)(2,1)}) %all-gather.5.cloned.1.call-update) | async-done | bytes 2097168 | tf_op jit(solution)/shard_map/all_gather | solution.py:20
  363.5 2.3 fusion.73
  365.8 1.9 fusion.6
  367.7 0.9 fusion.28
  368.7 0.9 broadcast_in_dim.22
  369.6 24.2 %all-to-all-start.2 = ((bf16[16,128,128]{2,1,0:T(8,128)(2,1)}), bf16[16,128,128]{2,1,0:T(8,128)(2,1)}, u32[]{:S(2)}, u32[]{:S(2)}) async-start(bf16[16,128,128]{2,1,0:T(8,128)(2,1)} %broadcast_in_dim.22), calls=%async_computation.2 | async-start | bytes 1048576 | tf_op jit(solution)/shard_map/all_to_all | solution.py:26
  393.8 2.0 fusion.21
  395.8 0.1 reduce_sum.188
  395.9 13.0 %all-to-all-done.2 = bf16[16,128,128]{2,1,0:T(8,128)(2,1)} async-done(((bf16[16,128,128]{2,1,0:T(8,128)(2,1)}), bf16[16,128,128]{2,1,0:T(8,128)(2,1)}, u32[]{:S(2)}, u32[]{:S(2)}) %all-to-all-start.2) | async-done | bytes 524320 | tf_op jit(solution)/shard_map/all_to_all | solution.py:26
  408.9 1.5 fusion.20
  410.4 0.1 reduce_sum.187
  410.5 0.7 fusion.56
  411.2 0.1 select_reduce_fusion
  411.3 11.7 %psum.35 = f32[2]{0:T(128)S(1)} all-reduce(f32[2]{0:T(128)S(1)} %select_reduce_fusion), channel_id=1, replica_groups=mesh['seq_0'=4,'seq_1'=8,'tp_0'=4,'tp_1'=2,'tp_2'=2] {'seq_0'}, use_global_device_ids=true, to_apply=%region_20.21 | all-reduce | flops 2 | bytes 16 | tf_op jit(solution)/shard_map/psum | solution.py:43
  423.0 13.4 %psum.36 = f32[2]{0:T(128)S(1)} all-reduce(f32[2]{0:T(128)S(1)} %psum.35), channel_id=1, replica_groups=mesh['seq_0'=4,'seq_1'=8,'tp_0'=4,'tp_1'=2,'tp_2'=2] {'seq_1'}, use_global_device_ids=true, to_apply=%region_21.22 | all-reduce | flops 2 | bytes 16 | tf_op jit(solution)/shard_map/psum | solution.py:43
  436.4 6.6 %psum.37 = f32[2]{0:T(128)S(1)} all-reduce(f32[2]{0:T(128)S(1)} %psum.36), channel_id=1, replica_groups=mesh['seq_0'=4,'seq_1'=8,'tp_0'=4,'tp_1'=2,'tp_2'=2] {'tp_0'}, use_global_device_ids=true, to_apply=%region_22.23 | all-reduce | flops 2 | bytes 16 | tf_op jit(solution)/shard_map/psum | solution.py:43
  443.0 7.7 %psum.38 = f32[2]{0:T(128)S(1)} all-reduce(f32[2]{0:T(128)S(1)} %psum.37), channel_id=1, replica_groups=mesh['seq_0'=4,'seq_1'=8,'tp_0'=4,'tp_1'=2,'tp_2'=2] {'tp_1'}, use_global_device_ids=true, to_apply=%region_23.24 | all-reduce | flops 2 | bytes 16 | tf_op jit(solution)/shard_map/psum | solution.py:43
  450.7 12.1 %psum.39 = f32[2]{0:T(128)S(1)} all-reduce(f32[2]{0:T(128)S(1)} %psum.38), channel_id=1, replica_groups=mesh['seq_0'=4,'seq_1'=8,'tp_0'=4,'tp_1'=2,'tp_2'=2] {'tp_2'}, use_global_device_ids=true, to_apply=%region_24.25 | all-reduce | flops 2 | bytes 16 | tf_op jit(solution)/shard_map/psum | solution.py:43
  462.7 0.6 fusion.63
  (46 shorter events, 0.8 us)
Async XLA Ops:
  7.2 50.1 %copy-start = (bf16[3072,128]{1,0:T(8,128)(2,1)S(1)}, bf16[3072,128]{1,0:T(8,128)(2,1)}, u32[]{:S(2)}) copy-start(bf16[3072,128]{1,0:T(8,128)(2,1)} %param.16) | copy-start | bytes 2359300
  7.2 49.6 %copy-start.2 = (bf16[3072,128]{1,0:T(8,128)(2,1)S(1)}, bf16[3072,128]{1,0:T(8,128)(2,1)}, u32[]{:S(2)}) copy-start(bf16[3072,128]{1,0:T(8,128)(2,1)} %param.17) | copy-start | bytes 2359300
  7.2 157.1 %all-gather.3.cloned.1.call-start = ((), (), s32[]{:S(2)}) async-start(), calls=%async_computation.4 | async-start | bytes 2162688 | tf_op jit(solution)/shard_map/all_gather | solution.py:20
  55.6 2.1 copy-start.6
  56.8 1.6 copy-start.1
  58.4 105.9 %copy-start.9 = (f32[128]{0:T(128)S(1)}, f32[128]{0:T(128)}, u32[]{:S(2)}) copy-start(f32[128]{0:T(128)} %param.19) | copy-start | bytes 1540
  59.6 109.9 %all-to-all-start.1 = ((bf16[128,16,192]{0,2,1:T(8,128)(2,1)}), bf16[128,16,192]{0,2,1:T(8,128)(2,1)S(1)}, u32[]{:S(2)}, u32[]{:S(2)}) async-start(bf16[128,16,192]{0,2,1:T(8,128)(2,1)} %bitcast.9), calls=%async_computation.1 | async-start | bytes 1572864 | tf_op jit(solution)/shard_map/all_to_all | solution.py:134
  164.3 4.2 copy-start.8
  170.5 42.8 %copy-start.3 = (bf16[128,192]{0,1:T(8,128)(2,1)S(1)}, bf16[128,192]{0,1:T(8,128)(2,1)}, u32[]{:S(2)}) copy-start(bf16[128,192]{0,1:T(8,128)(2,1)} %param.11) | copy-start | bytes 147460
  170.5 41.2 %all-to-all-start = ((bf16[16,128,128]{2,1,0:T(8,128)(2,1)}), bf16[16,128,128]{2,1,0:T(8,128)(2,1)}, u32[]{:S(2)}, u32[]{:S(2)}) async-start(bf16[16,128,128]{2,1,0:T(8,128)(2,1)} %broadcast_in_dim.20), calls=%async_computation | async-start | bytes 1048576 | tf_op jit(solution)/shard_map/all_to_all | solution.py:26
  195.6 167.9 %all-gather.5.cloned.1.call-start = ((), (), s32[]{:S(2)}) async-start(), calls=%async_computation.5 | async-start | bytes 2162688 | tf_op jit(solution)/shard_map/all_gather | solution.py:20
  195.6 51.7 %copy-start.5 = (f32[3072]{0:T(1024)S(1)}, f32[3072]{0:T(1024)}, u32[]{:S(2)}) copy-start(f32[3072]{0:T(1024)} %param.14) | copy-start | bytes 36868
  253.5 115.2 %all-to-all-start.3 = ((bf16[192,16,192]{0,2,1:T(8,128)(2,1)}), bf16[192,16,192]{0,2,1:T(8,128)(2,1)}, u32[]{:S(2)}, u32[]{:S(2)}) async-start(bf16[192,16,192]{0,2,1:T(8,128)(2,1)} %bitcast.82), calls=%async_computation.3 | async-start | bytes 3145728 | tf_op jit(solution)/shard_map/all_to_all | solution.py:135
  363.5 4.2 copy-start.7
  369.6 39.2 %all-to-all-start.2 = ((bf16[16,128,128]{2,1,0:T(8,128)(2,1)}), bf16[16,128,128]{2,1,0:T(8,128)(2,1)}, u32[]{:S(2)}, u32[]{:S(2)}) async-start(bf16[16,128,128]{2,1,0:T(8,128)(2,1)} %broadcast_in_dim.22), calls=%async_computation.2 | async-start | bytes 1048576 | tf_op jit(solution)/shard_map/all_to_all | solution.py:26
  395.8 67.0 %copy-start.10 = (s32[2]{0:T(128)S(1)}, s32[2]{0:T(128)}, u32[]{:S(2)}) copy-start(s32[2]{0:T(128)} %param.12) | copy-start | bytes 28
  395.9 68.1 %copy-start.4 = (bf16[128,192]{0,1:T(8,128)(2,1)}, bf16[128,192]{0,1:T(8,128)(2,1)S(1)}, u32[]{:S(2)}) copy-start(bf16[128,192]{0,1:T(8,128)(2,1)S(1)} %reduce_sum.188) | copy-start | bytes 147460
Sparse Core Ops, SparseCore 0:
  58.5 105.7 all-gather.2
  251.1 112.4 all-gather.4
where the time goes:
time: 473 us; the launch traced here: 472 us
  waiting for transfers between devices  227 us (48%)
  blocking collectives  131 us (28%)
  starting transfers between devices  62.3 us (13%)
  matrix products  18.5 us (4%)
  between operations  16.1 us (3%)
  other arithmetic  10.8 us (2%)
  local copies, waits for them, and re-layouts  5.83 us (1%)
    all_gather x2, waiting for transfers between devices, in_one_piece(): whole = lax.all_gather(both, axis, axis=dim, tiled=True)  198 us
    psum x5, blocking collectives, over_axes(): return functools.reduce(lax.psum, axes, value)  51.4 us
    all_to_all x2, starting transfers between devices, from_everyone(): lax.all_to_all(jnp.broadcast_to(value[None], (length, *value.shape)), axi...  49.3 us
    all_gather x1, blocking collectives, on_device(): whole_rows = lax.all_gather(latents, TP, axis=1, tiled=True)  46.2 us
    all_gather x1, blocking collectives, on_device(): whole_rows = lax.all_gather(state_shard, TP, axis=1, tiled=True)  33.6 us
    all_to_all x2, waiting for transfers between devices, from_everyone(): lax.all_to_all(jnp.broadcast_to(value[None], (length, *value.shape)), axi...  29 us
  transfers between devices with their start and end apart: 6, of which 4 were waited for; matrix products, arithmetic and copies ran while one was open for 4% of the time, Pallas kernels for 0%

commit v1 on v0

--- a/solution.py
+++ b/solution.py
@@ -127,7 +127,7 @@
     ).astype(jnp.float32)
     start_times = jnp.sum(one_hot * (t_index.astype(jnp.float32) / TGRID)[None, :], axis=1)
     step_size = 1.0 / TGRID
-    whole_rows = lax.all_gather(latents, TP, axis=1, tiled=True)
+    whole_rows = jnp.concatenate(lax.all_gather(latents, TP), axis=1)
     velocities = []
     first_hidden = whole_rows
     out_columns, student_columns = (

time: 473 us -> 471 us (level)
  no operation moved by 1% of the time
where the time goes in v1:
time: 471 us; the launch traced here: 470 us
  waiting for transfers between devices  230 us (49%)
  blocking collectives  130 us (28%)
  starting transfers between devices  62.9 us (13%)
  between operations  16.4 us (3%)
  matrix products  15.2 us (3%)
  other arithmetic  9.84 us (2%)
  local copies, waits for them, and re-layouts  6.34 us (1%)
    all_gather x2, waiting for transfers between devices, in_one_piece(): whole = lax.all_gather(both, axis, axis=dim, tiled=True)  202 us
    all_to_all x2, starting transfers between devices, from_everyone(): lax.all_to_all(jnp.broadcast_to(value[None], (length, *value.shape)), axi...  49.8 us
    psum x5, blocking collectives, over_axes(): return functools.reduce(lax.psum, axes, value)  49.6 us
    all_gather x1, blocking collectives, on_device(): whole_rows = jnp.concatenate(lax.all_gather(latents, TP), axis=1)  46.1 us
    all_gather x1, blocking collectives, on_device(): whole_rows = lax.all_gather(state_shard, TP, axis=1, tiled=True)  34.3 us
    all_to_all x2, waiting for transfers between devices, from_everyone(): lax.all_to_all(jnp.broadcast_to(value[None], (length, *value.shape)), axi...  27.9 us
  transfers between devices with their start and end apart: 6, of which 4 were waited for; matrix products, arithmetic and copies ran while one was open for 4% of the time, Pallas kernels for 0%

profile of v1, /device:TPU:1, one launch (start us, length us, event | category | flops | bytes accessed | tf_op | source)
XLA Modules:
  0.0 470.3 jit_solution(896981106944623310)
XLA Ops:
  7.2 0.7 convert_multiply_fusion.4
  8.0 46.1 %all-gather = bf16[2048,192]{0,1:T(8,128)(2,1)S(1)} all-gather(bf16[128,192]{0,1:T(8,128)(2,1)} %param.11), channel_id=2, replica_groups=mesh['seq_0'=4,'seq_1'=8,'tp_0'=4,'tp_1'=2,'tp_2'=2] {'tp_0','tp_1','tp_2'}, dimensions={0}, use_global_device_ids=true | all-gather | bytes 835584 | tf_op jit(solution)/shard_map/all_gather | solution.py:130
  54.0 0.4 convert_bitcast_fusion
  54.4 0.3 copy.27
  54.7 0.4 fusion.11
  55.2 0.4 copy-done.1
  55.6 0.1 copy.32
  55.7 0.5 copy-done.26
  56.2 0.2 reduce-window.8
  56.6 0.5 fusion.13
  57.1 1.6 convolution_convert_fusion.3
  58.7 0.4 multiply_reduce_fusion.3
  59.3 0.6 pad_maximum_fusion
  59.9 1.2 copy.22
  61.1 3.7 all-to-all-start.1
  64.8 0.4 multiply_reduce_fusion.2
  65.4 100.7 %all-gather.4.cloned.1.call-done = bf16[4096,256]{0,1:T(8,128)(2,1)} async-done(((bf16[128,256]{0,1:T(8,128)(2,1)}), bf16[4096,256]{0,1:T(8,128)(2,1)}) %all-gather.4.cloned.1.call-update) | async-done | bytes 2097168 | tf_op jit(solution)/shard_map/all_gather | solution.py:20
  166.1 2.1 fusion.79
  168.2 1.9 fusion.4
  170.1 0.9 fusion.30
  171.1 0.9 broadcast_in_dim.20
  172.0 24.8 %all-to-all-start = ((bf16[16,128,128]{2,1,0:T(8,128)(2,1)}), bf16[16,128,128]{2,1,0:T(8,128)(2,1)S(1)}, u32[]{:S(2)}, u32[]{:S(2)}) async-start(bf16[16,128,128]{2,1,0:T(8,128)(2,1)} %broadcast_in_dim.20), calls=%async_computation | async-start | bytes 1048576 | tf_op jit(solution)/shard_map/all_to_all | solution.py:26
  196.9 15.4 %all-to-all-done = bf16[16,128,128]{2,1,0:T(8,128)(2,1)S(1)} async-done(((bf16[16,128,128]{2,1,0:T(8,128)(2,1)}), bf16[16,128,128]{2,1,0:T(8,128)(2,1)S(1)}, u32[]{:S(2)}, u32[]{:S(2)}) %all-to-all-start) | async-done | bytes 524320 | tf_op jit(solution)/shard_map/all_to_all | solution.py:26
  212.3 0.5 fusion.20
  212.9 34.3 %all_gather.18 = bf16[128,3072]{0,1:T(8,128)(2,1)S(1)} all-gather(bf16[128,192]{0,1:T(8,128)(2,1)S(1)} %fusion.57), channel_id=1, replica_groups=mesh['seq_0'=4,'seq_1'=8,'tp_0'=4,'tp_1'=2,'tp_2'=2] {'tp_0','tp_1','tp_2'}, dimensions={1}, use_global_device_ids=true | all-gather | bytes 835584 | tf_op jit(solution)/shard_map/all_gather | solution.py:140
  247.2 0.4 fusion.8
  247.7 0.8 convolution_convert_fusion.2
  248.6 1.6 multiply_reduce_fusion.1
  250.3 0.6 pad_maximum_fusion.1
  250.9 1.6 copy.25
  252.5 9.3 %all-to-all-start.3 = ((bf16[192,16,192]{0,2,1:T(8,128)(2,1)}), bf16[192,16,192]{0,2,1:T(8,128)(2,1)}, u32[]{:S(2)}, u32[]{:S(2)}) async-start(bf16[192,16,192]{0,2,1:T(8,128)(2,1)} %bitcast.109), calls=%async_computation.3 | async-start | bytes 3145728 | tf_op jit(solution)/shard_map/all_to_all | solution.py:135
  261.9 0.9 multiply_reduce_fusion
  262.7 101.1 %all-gather.6.cloned.1.call-done = bf16[4096,256]{0,1:T(8,128)(2,1)} async-done(((bf16[128,256]{0,1:T(8,128)(2,1)}), bf16[4096,256]{0,1:T(8,128)(2,1)}) %all-gather.6.cloned.1.call-update) | async-done | bytes 2097168 | tf_op jit(solution)/shard_map/all_gather | solution.py:20
  363.8 2.1 fusion.80
  366.0 1.9 fusion.6
  367.8 0.9 fusion.29
  368.9 0.9 broadcast_in_dim.22
  369.8 25.0 %all-to-all-start.2 = ((bf16[16,128,128]{2,1,0:T(8,128)(2,1)}), bf16[16,128,128]{2,1,0:T(8,128)(2,1)S(1)}, u32[]{:S(2)}, u32[]{:S(2)}) async-start(bf16[16,128,128]{2,1,0:T(8,128)(2,1)} %broadcast_in_dim.22), calls=%async_computation.2 | async-start | bytes 1048576 | tf_op jit(solution)/shard_map/all_to_all | solution.py:26
  394.9 2.6 fusion.22
  397.6 12.5 %all-to-all-done.2 = bf16[16,128,128]{2,1,0:T(8,128)(2,1)S(1)} async-done(((bf16[16,128,128]{2,1,0:T(8,128)(2,1)}), bf16[16,128,128]{2,1,0:T(8,128)(2,1)S(1)}, u32[]{:S(2)}, u32[]{:S(2)}) %all-to-all-start.2) | async-done | bytes 524320 | tf_op jit(solution)/shard_map/all_to_all | solution.py:26
  410.1 0.5 fusion.21
  410.7 0.7 fusion.62
  411.5 10.2 %psum.35 = f32[2]{0:T(128)S(1)} all-reduce(f32[2]{0:T(128)S(1)} %select_reduce_fusion), channel_id=1, replica_groups=mesh['seq_0'=4,'seq_1'=8,'tp_0'=4,'tp_1'=2,'tp_2'=2] {'seq_0'}, use_global_device_ids=true, to_apply=%region_20.21 | all-reduce | flops 2 | bytes 16 | tf_op jit(solution)/shard_map/psum | solution.py:43
  421.7 13.2 %psum.36 = f32[2]{0:T(128)S(1)} all-reduce(f32[2]{0:T(128)S(1)} %psum.35), channel_id=1, replica_groups=mesh['seq_0'=4,'seq_1'=8,'tp_0'=4,'tp_1'=2,'tp_2'=2] {'seq_1'}, use_global_device_ids=true, to_apply=%region_21.22 | all-reduce | flops 2 | bytes 16 | tf_op jit(solution)/shard_map/psum | solution.py:43
  434.9 6.6 %psum.37 = f32[2]{0:T(128)S(1)} all-reduce(f32[2]{0:T(128)S(1)} %psum.36), channel_id=1, replica_groups=mesh['seq_0'=4,'seq_1'=8,'tp_0'=4,'tp_1'=2,'tp_2'=2] {'tp_0'}, use_global_device_ids=true, to_apply=%region_22.23 | all-reduce | flops 2 | bytes 16 | tf_op jit(solution)/shard_map/psum | solution.py:43
  441.5 7.7 %psum.38 = f32[2]{0:T(128)S(1)} all-reduce(f32[2]{0:T(128)S(1)} %psum.37), channel_id=1, replica_groups=mesh['seq_0'=4,'seq_1'=8,'tp_0'=4,'tp_1'=2,'tp_2'=2] {'tp_1'}, use_global_device_ids=true, to_apply=%region_23.24 | all-reduce | flops 2 | bytes 16 | tf_op jit(solution)/shard_map/psum | solution.py:43
  449.2 11.9 %psum.39 = f32[2]{0:T(128)S(1)} all-reduce(f32[2]{0:T(128)S(1)} %psum.38), channel_id=1, replica_groups=mesh['seq_0'=4,'seq_1'=8,'tp_0'=4,'tp_1'=2,'tp_2'=2] {'tp_2'}, use_global_device_ids=true, to_apply=%region_24.25 | all-reduce | flops 2 | bytes 16 | tf_op jit(solution)/shard_map/psum | solution.py:43
  461.1 0.6 fusion.69
  (92 shorter events, 1.6 us)
Async XLA Ops:
  7.2 51.6 %copy-start = (bf16[3072,128]{1,0:T(8,128)(2,1)S(1)}, bf16[3072,128]{1,0:T(8,128)(2,1)}, u32[]{:S(2)}) copy-start(bf16[3072,128]{1,0:T(8,128)(2,1)} %param.16) | copy-start | bytes 2359300
  7.2 158.9 %all-gather.4.cloned.1.call-start = ((), (), s32[]{:S(2)}) async-start(), calls=%async_computation.4 | async-start | bytes 2162688 | tf_op jit(solution)/shard_map/all_gather | solution.py:20
  54.4 1.2 copy-start.1
  55.2 1.4 copy-start.18
  55.6 0.7 copy-start.26
  55.6 1.0 copy-start.11
  56.5 113.6 %copy-start.16 = (s32[128]{0:T(128)}, s32[128]{0:T(128)S(1)}, u32[]{:S(2)}) copy-start(s32[128]{0:T(128)S(1)} %fusion.68) | copy-start | bytes 1540
  56.6 140.3 %copy-start.20 = (f32[128]{0:T(128)}, f32[128]{0:T(128)S(1)}, u32[]{:S(2)}) copy-start(f32[128]{0:T(128)S(1)} %select_reduce_fusion.1) | copy-start | bytes 1540
  57.1 2.1 copy-start.14
  57.1 2.8 copy-start.3
  59.9 4.9 %copy-start.5 = (bf16[3072,128]{1,0:T(8,128)(2,1)S(1)}, bf16[3072,128]{1,0:T(8,128)(2,1)}, u32[]{:S(2)}) copy-start(bf16[3072,128]{1,0:T(8,128)(2,1)} %param.15) | copy-start | bytes 2359300
  61.1 104.9 %copy-start.24 = (f32[128]{0:T(128)S(1)}, f32[128]{0:T(128)}, u32[]{:S(2)}) copy-start(f32[128]{0:T(128)} %param.19) | copy-start | bytes 1540
  61.1 110.0 %all-to-all-start.1 = ((bf16[128,16,192]{0,2,1:T(8,128)(2,1)}), bf16[128,16,192]{0,2,1:T(8,128)(2,1)S(1)}, u32[]{:S(2)}, u32[]{:S(2)}) async-start(bf16[128,16,192]{0,2,1:T(8,128)(2,1)} %bitcast.11), calls=%async_computation.1 | async-start | bytes 1572864 | tf_op jit(solution)/shard_map/all_to_all | solution.py:134
  168.2 1.9 copy-start.23
  172.0 40.3 %all-to-all-start = ((bf16[16,128,128]{2,1,0:T(8,128)(2,1)}), bf16[16,128,128]{2,1,0:T(8,128)(2,1)S(1)}, u32[]{:S(2)}, u32[]{:S(2)}) async-start(bf16[16,128,128]{2,1,0:T(8,128)(2,1)} %broadcast_in_dim.20), calls=%async_computation | async-start | bytes 1048576 | tf_op jit(solution)/shard_map/all_to_all | solution.py:26
  196.8 16.1 %copy-start.9 = (bf16[128,192]{0,1:T(8,128)(2,1)S(1)}, bf16[128,192]{0,1:T(8,128)(2,1)}, u32[]{:S(2)}) copy-start(bf16[128,192]{0,1:T(8,128)(2,1)} %param.11) | copy-start | bytes 147460
  196.8 167.0 %all-gather.6.cloned.1.call-start = ((), (), s32[]{:S(2)}) async-start(), calls=%async_computation.5 | async-start | bytes 2162688 | tf_op jit(solution)/shard_map/all_gather | solution.py:20
  196.9 50.8 %copy-start.28 = (f32[128]{0:T(128)}, f32[128]{0:T(128)S(1)}, u32[]{:S(2)}) copy-start(f32[128]{0:T(128)S(1)} %broadcast_add_fusion) | copy-start | bytes 1540
  212.7 34.9 %copy-start.4 = (bf16[3072,128]{1,0:T(8,128)(2,1)S(1)}, bf16[3072,128]{1,0:T(8,128)(2,1)}, u32[]{:S(2)}) copy-start(bf16[3072,128]{1,0:T(8,128)(2,1)} %param.17) | copy-start | bytes 2359300
  212.9 34.8 %copy-start.7 = (bf16[128,192]{0,1:T(8,128)(2,1)}, bf16[128,192]{0,1:T(8,128)(2,1)S(1)}, u32[]{:S(2)}) copy-start(bf16[128,192]{0,1:T(8,128)(2,1)S(1)} %reduce_sum.182) | copy-start | bytes 147460
  247.7 0.9 copy-start.12
  247.7 2.4 copy-start.30
  248.6 1.6 copy-start.15
  248.6 2.3 copy-start.2
  252.5 9.3 %copy-start.6 = (bf16[3072,128]{1,0:T(8,128)(2,1)S(1)}, bf16[3072,128]{1,0:T(8,128)(2,1)}, u32[]{:S(2)}) copy-start(bf16[3072,128]{1,0:T(8,128)(2,1)} %param.15) | copy-start | bytes 2359300
  252.5 9.3 %copy-start.13 = (f32[3072]{0:T(1024)S(1)}, f32[3072]{0:T(1024)}, u32[]{:S(2)}) copy-start(f32[3072]{0:T(1024)} %param.14) | copy-start | bytes 36868
  252.5 9.3 %copy-start.29 = (f32[128]{0:T(128)S(1)}, f32[128]{0:T(128)}, u32[]{:S(2)}) copy-start(f32[128]{0:T(128)} %copy-done.28) | copy-start | bytes 1540
  252.5 9.3 %copy-start.31 = (f32[128]{0:T(128)S(1)}, f32[128]{0:T(128)}, u32[]{:S(2)}) copy-start(f32[128]{0:T(128)} %copy-done.30) | copy-start | bytes 1540
  252.5 116.3 %all-to-all-start.3 = ((bf16[192,16,192]{0,2,1:T(8,128)(2,1)}), bf16[192,16,192]{0,2,1:T(8,128)(2,1)}, u32[]{:S(2)}, u32[]{:S(2)}) async-start(bf16[192,16,192]{0,2,1:T(8,128)(2,1)} %bitcast.109), calls=%async_computation.3 | async-start | bytes 3145728 | tf_op jit(solution)/shard_map/all_to_all | solution.py:135
  261.8 102.0 %copy-start.17 = (s32[128]{0:T(128)S(1)}, s32[128]{0:T(128)}, u32[]{:S(2)}) copy-start(s32[128]{0:T(128)} %copy-done.16) | copy-start | bytes 1540
  261.8 101.9 %copy-start.25 = (f32[128]{0:T(128)S(1)}, f32[128]{0:T(128)}, u32[]{:S(2)}) copy-start(f32[128]{0:T(128)} %param.19) | copy-start | bytes 1540
  365.9 1.9 copy-start.22
  368.7 26.2 %copy-start.19 = (f32[128]{0:T(128)S(1)}, f32[128]{0:T(128)}, u32[]{:S(2)}) copy-start(f32[128]{0:T(128)} %copy-done.18) | copy-start | bytes 1540
  368.7 26.2 %copy-start.21 = (f32[128]{0:T(128)S(1)}, f32[128]{0:T(128)}, u32[]{:S(2)}) copy-start(f32[128]{0:T(128)} %copy-done.20) | copy-start | bytes 1540
  369.8 40.3 %all-to-all-start.2 = ((bf16[16,128,128]{2,1,0:T(8,128)(2,1)}), bf16[16,128,128]{2,1,0:T(8,128)(2,1)S(1)}, u32[]{:S(2)}, u32[]{:S(2)}) async-start(bf16[16,128,128]{2,1,0:T(8,128)(2,1)} %broadcast_in_dim.22), calls=%async_computation.2 | async-start | bytes 1048576 | tf_op jit(solution)/shard_map/all_to_all | solution.py:26
  397.6 51.6 %copy-start.10 = (bf16[128,192]{0,1:T(8,128)(2,1)}, bf16[128,192]{0,1:T(8,128)(2,1)S(1)}, u32[]{:S(2)}) copy-start(bf16[128,192]{0,1:T(8,128)(2,1)S(1)} %reduce_sum.188) | copy-start | bytes 147460
  397.6 13.1 %copy-start.8 = (bf16[128,192]{0,1:T(8,128)(2,1)S(1)}, bf16[128,192]{0,1:T(8,128)(2,1)}, u32[]{:S(2)}) copy-start(bf16[128,192]{0,1:T(8,128)(2,1)} %copy-done.7) | copy-start | bytes 147460
  397.6 63.5 %copy-start.27 = (s32[2]{0:T(128)S(1)}, s32[2]{0:T(128)}, u32[]{:S(2)}) copy-start(s32[2]{0:T(128)} %param.12) | copy-start | bytes 28
Sparse Core Ops, SparseCore 0:
  60.0 105.9 all-gather.3
  251.0 112.7 all-gather.5
